TPU v7x, 32 devices: a whole 2x2x4 slice. The times are simulated.
32 devices in a mesh: dp: 8 (over z, core), fsdp: 4 (over y, x).
Axes of the slice: x: 2, y: 2, z: 4, core: 2. Of those that a mesh axis runs over, the one named last changes fastest.
Arguments:
- inputs: bfloat16 [64, 512, 768], P(('dp', 'fsdp')), may hold values from -6 to 6
- segment_ids: int32 [64, 512], P(('dp', 'fsdp')), may hold values from 0 to 3, never falling along the last dimension, each value on 1 to 256 neighbouring positions
- cotangent: bfloat16 [64, 512, 768], P(('dp', 'fsdp')), may hold values from -9 to 9
- qkv_weight: bfloat16 [768, 2304], P(('dp', 'fsdp')), may hold values from -0.21875 to 0.21875
- out_weight: bfloat16 [768, 768], P(('dp', 'fsdp')), may hold values from -1.75 to 1.75
- up_weight: bfloat16 [768, 3072], P(('dp', 'fsdp')), may hold values from -0.21875 to 0.21875
- down_weight: bfloat16 [3072, 768], P(('dp', 'fsdp')), may hold values from -0.109375 to 0.109375
- query_bias_vector: bfloat16 [768], P(('dp', 'fsdp')), may hold values from -1.5 to 1.5
- value_bias_vector: bfloat16 [768], P(('dp', 'fsdp')), may hold values from -1.5 to 1.5
- out_bias: bfloat16 [768], P(('dp', 'fsdp')), may hold values from -1.5 to 1.5
- gain_one: bfloat16 [768], P(('dp', 'fsdp')), may hold values from 0.5 to 1.5
- shift_one: bfloat16 [768], P(('dp', 'fsdp')), may hold values from -1.5 to 1.5
- up_bias: bfloat16 [3072], P(('dp', 'fsdp')), may hold values from -1.5 to 1.5
- down_bias: bfloat16 [768], P(('dp', 'fsdp')), may hold values from -1.5 to 1.5
- gain_two: bfloat16 [768], P(('dp', 'fsdp')), may hold values from 0.5 to 1.5
- shift_two: bfloat16 [768], P(('dp', 'fsdp')), may hold values from -1.5 to 1.5
- query_down: bfloat16 [768, 8], replicated, may hold values from -0.21875 to 0.21875
- query_up_weight: bfloat16 [8, 768], replicated, may hold values from -2 to 2
- value_down: bfloat16 [768, 8], replicated, may hold values from -0.21875 to 0.21875
- value_up_weight: bfloat16 [8, 768], replicated, may hold values from -2 to 2
Outputs:
- output: bfloat16 [64, 512, 768], P(('dp', 'fsdp'))
- grad_input: float32 [64, 512, 768], P(('dp', 'fsdp'))
- grad_query_down: float32 [768, 8], replicated
- grad_query_up: float32 [8, 768], replicated
- grad_value_down: float32 [768, 8], replicated
- grad_value_up: float32 [8, 768], replicated
Inputs may be any that keep to these rules, and one draw needn't show every extreme that they name: `segment_ids`: within a pack the ids never fall; each of the 4 documents has 1 to 256 rows, and one has exactly 256.
All inputs are finite; a program needn't handle non-finite values.
Results may differ from a plain program's by a relative error of at most 0.015.
The roundings to bfloat16 on the way count: a program that leaves them out, or rounds other values in their place, can miss the bound.
Values may be sent and summed in bfloat16 or wider, within the bound.
No kernel may reach another device: no remote copies, remote signals or barrier semaphores. Data moves between devices by JAX's collectives and lax.ppermute only.
A program may use at most 128 MiB of HBM per device.

v0:
```python
from functools import partial
import jax
import jax.numpy as jnp
from jax import lax
from jax.sharding import PartitionSpec as P

HEADS = 12
HEAD_DIM = 64
highest_precision_mode = lax.Precision.HIGHEST
norm_epsilon = 1e-05
adapter_scale = 2.0


def layer_norm(value_rows, gain, shift):
    centred = value_rows - jnp.mean(value_rows, axis=-1, keepdims=True)
    variance = jnp.mean(centred * centred, axis=-1, keepdims=True)
    return centred * lax.rsqrt(variance + norm_epsilon) * gain + shift


def gelu_exact(value_rows):
    return jax.nn.gelu(value_rows, approximate=False)


def fetch_forward(qkv_weight, out_weight, up_weight, down_weight, vectors, up_bias):
    return (
        lax.all_gather(qkv_weight, ("dp", "fsdp"), axis=0, tiled=True),
        lax.all_gather(out_weight, ("dp", "fsdp"), axis=0, tiled=True),
        lax.all_gather(up_weight, ("dp", "fsdp"), axis=0, tiled=True),
        lax.all_gather(down_weight, ("dp", "fsdp"), axis=0, tiled=True),
        lax.all_gather(vectors, ("dp", "fsdp"), axis=1, tiled=True),
        lax.all_gather(up_bias, ("dp", "fsdp"), axis=0, tiled=True),
    )


def fetch_backward(qkv_weight, out_weight, up_weight, down_weight, gains):
    return (
        lax.all_gather(qkv_weight, ("dp", "fsdp"), axis=0, tiled=True),
        lax.all_gather(out_weight, ("dp", "fsdp"), axis=0, tiled=True),
        lax.all_gather(up_weight, ("dp", "fsdp"), axis=0, tiled=True),
        lax.all_gather(down_weight, ("dp", "fsdp"), axis=0, tiled=True),
        lax.all_gather(gains, ("dp", "fsdp"), axis=1, tiled=True),
    )


def segment_mask(segment):
    return (segment[:, None] == segment[None, :])[None]


def attend_pack(packed):
    query_rows, key_rows, value_rows, segment = packed
    scale = query_rows.shape[-1] ** (-0.5)
    raw_scores = jnp.einsum(
        "qhd,khd->hqk", query_rows, key_rows, preferred_element_type=jnp.float32
    )
    in_segment = segment_mask(segment)
    masked = jnp.where(in_segment, raw_scores * scale, -jnp.inf)
    highest = jnp.max(masked, axis=-1, keepdims=True)
    exponent = jnp.where(in_segment, jnp.exp(masked - highest), 0.0)
    row_total = jnp.sum(exponent, axis=-1, keepdims=True)
    probs_low = (exponent / row_total).astype(jnp.bfloat16)
    attended = jnp.einsum("hqk,khd->qhd", probs_low, value_rows, preferred_element_type=jnp.float32)
    return (attended, (highest + jnp.log(row_total))[..., 0])


def attend_back(packed):
    query_rows, key_rows, value_rows, segment, log_total, grad_mixed = packed
    scale = query_rows.shape[-1] ** (-0.5)
    raw_scores = jnp.einsum(
        "qhd,khd->hqk", query_rows, key_rows, preferred_element_type=jnp.float32
    )
    in_segment = segment_mask(segment)
    probs = jnp.where(in_segment, jnp.exp(raw_scores * scale - log_total[..., None]), 0.0)
    value_rows_gradient = jnp.einsum(
        "hqk,qhd->khd", probs.astype(jnp.bfloat16), grad_mixed, preferred_element_type=jnp.float32
    )
    grad_probs = jnp.einsum(
        "qhd,khd->hqk", grad_mixed, value_rows, preferred_element_type=jnp.float32
    )
    inner_sum = jnp.sum(probs * grad_probs, axis=-1, keepdims=True)
    grad_raw = (probs * (grad_probs - inner_sum) * scale).astype(jnp.bfloat16)
    query_rows_gradient = jnp.einsum(
        "hqk,khd->qhd", grad_raw, key_rows, preferred_element_type=jnp.float32
    )
    grad_keys = jnp.einsum("hqk,qhd->khd", grad_raw, query_rows, preferred_element_type=jnp.float32)
    return (
        query_rows_gradient.astype(jnp.bfloat16),
        grad_keys.astype(jnp.bfloat16),
        value_rows_gradient.astype(jnp.bfloat16),
    )


def local(
    inputs,
    segment_ids,
    cotangent,
    qkv_weight,
    out_weight,
    up_weight,
    down_weight,
    query_bias_vector,
    value_bias_vector,
    out_bias,
    gain_one,
    shift_one,
    up_bias,
    down_bias,
    gain_two,
    shift_two,
    query_down,
    query_up_weight,
    value_down,
    value_up_weight,
):
    vector_shards = jnp.stack(
        [
            query_bias_vector,
            value_bias_vector,
            out_bias,
            gain_one,
            shift_one,
            down_bias,
            gain_two,
            shift_two,
        ]
    )
    qkv_full, out_full, up_full, down_full, vector_full, up_bias_full = fetch_forward(
        qkv_weight, out_weight, up_weight, down_weight, vector_shards, up_bias
    )
    vectors = vector_full.astype(jnp.float32)
    packs, seq_len, width = inputs.shape
    rows = packs * seq_len
    flat_in = inputs.reshape(rows, width)
    flat_float = flat_in.astype(jnp.float32)
    projected_rows = jnp.dot(flat_in, qkv_full, preferred_element_type=jnp.float32)
    query_rank_rows = jnp.dot(flat_in, query_down, preferred_element_type=jnp.float32)
    value_rank_rows = jnp.dot(flat_in, value_down, preferred_element_type=jnp.float32)
    query_up_weight_float = query_up_weight.astype(jnp.float32)
    value_up_weight_float = value_up_weight.astype(jnp.float32)
    query_rows = (
        projected_rows[:, :width]
        + vectors[0]
        + adapter_scale
        * jnp.dot(query_rank_rows, query_up_weight_float, precision=highest_precision_mode)
    ).astype(jnp.bfloat16)
    key_rows = projected_rows[:, width : 2 * width].astype(jnp.bfloat16)
    value_rows = (
        projected_rows[:, 2 * width :]
        + vectors[1]
        + adapter_scale
        * jnp.dot(value_rank_rows, value_up_weight_float, precision=highest_precision_mode)
    ).astype(jnp.bfloat16)
    head_shape = (packs, seq_len, HEADS, HEAD_DIM)
    queries_heads = query_rows.reshape(head_shape)
    keys_heads = key_rows.reshape(head_shape)
    values_heads = value_rows.reshape(head_shape)
    attended, log_total = lax.map(
        attend_pack, (queries_heads, keys_heads, values_heads, segment_ids)
    )
    attended_low = attended.reshape(rows, width).astype(jnp.bfloat16)
    hidden_one = (
        flat_float
        + jnp.dot(attended_low, out_full, preferred_element_type=jnp.float32)
        + vectors[2]
    )
    normed_one = layer_norm(hidden_one, vectors[3], vectors[4])
    upper = jnp.dot(
        normed_one.astype(jnp.bfloat16), up_full, preferred_element_type=jnp.float32
    ) + up_bias_full.astype(jnp.float32)
    activated, gelu_pull = jax.vjp(gelu_exact, upper)
    hidden_two = (
        normed_one
        + jnp.dot(activated.astype(jnp.bfloat16), down_full, preferred_element_type=jnp.float32)
        + vectors[5]
    )
    output = layer_norm(hidden_two, vectors[6], vectors[7]).astype(jnp.bfloat16)
    gain_shards = jnp.stack([gain_one, gain_two])
    qkv_back, out_back, up_back, down_back, gain_back = fetch_backward(
        qkv_weight, out_weight, up_weight, down_weight, gain_shards
    )
    gain_back = gain_back.astype(jnp.float32)
    gain_back_one, gain_back_two = (gain_back[0], gain_back[1])
    grad_out = cotangent.reshape(rows, width).astype(jnp.float32)
    normed_again, pull_two = jax.vjp(partial(layer_norm, gain=gain_back_two, shift=0.0), hidden_two)
    (grad_two,) = pull_two(grad_out)
    grad_act = jnp.dot(
        grad_two.astype(jnp.bfloat16), down_back.T, preferred_element_type=jnp.float32
    )
    (grad_upper,) = gelu_pull(grad_act)
    grad_normed = grad_two + jnp.dot(
        grad_upper.astype(jnp.bfloat16), up_back.T, preferred_element_type=jnp.float32
    )
    first_again, pull_one = jax.vjp(partial(layer_norm, gain=gain_back_one, shift=0.0), hidden_one)
    (grad_one,) = pull_one(grad_normed)
    grad_mixed = jnp.dot(
        grad_one.astype(jnp.bfloat16), out_back.T, preferred_element_type=jnp.float32
    ).astype(jnp.bfloat16)
    query_rows_gradient, grad_keys, value_rows_gradient = lax.map(
        attend_back,
        (
            queries_heads,
            keys_heads,
            values_heads,
            segment_ids,
            log_total,
            grad_mixed.reshape(head_shape),
        ),
    )
    query_rows_gradient = query_rows_gradient.reshape(rows, width)
    value_rows_gradient = value_rows_gradient.reshape(rows, width)
    grad_project = jnp.concatenate(
        [query_rows_gradient, grad_keys.reshape(rows, width), value_rows_gradient], axis=1
    )
    query_rank_gradient = adapter_scale * jnp.dot(
        query_rows_gradient, query_up_weight.T, preferred_element_type=jnp.float32
    )
    value_rank_gradient = adapter_scale * jnp.dot(
        value_rows_gradient, value_up_weight.T, preferred_element_type=jnp.float32
    )
    grad_rows = grad_one + jnp.dot(grad_project, qkv_back.T, preferred_element_type=jnp.float32)
    grad_rows = grad_rows + jnp.dot(
        query_rank_gradient, query_down.astype(jnp.float32).T, precision=highest_precision_mode
    )
    grad_rows = grad_rows + jnp.dot(
        value_rank_gradient, value_down.astype(jnp.float32).T, precision=highest_precision_mode
    )
    term_query_up = jnp.dot(
        query_rank_rows.T,
        adapter_scale * query_rows_gradient.astype(jnp.float32),
        precision=highest_precision_mode,
    )
    term_value_up = jnp.dot(
        value_rank_rows.T,
        adapter_scale * value_rows_gradient.astype(jnp.float32),
        precision=highest_precision_mode,
    )
    term_query_down = jnp.dot(flat_float.T, query_rank_gradient, precision=highest_precision_mode)
    term_value_down = jnp.dot(flat_float.T, value_rank_gradient, precision=highest_precision_mode)
    sum_query_down, sum_query_up, sum_value_down, sum_value_up = lax.psum(
        (term_query_down, term_query_up, term_value_down, term_value_up), ("dp", "fsdp")
    )
    return (
        output.reshape(packs, seq_len, width),
        grad_rows.reshape(packs, seq_len, width),
        sum_query_down,
        sum_query_up,
        sum_value_down,
        sum_value_up,
    )


def solution(mesh):
    in_specs = (
        P(("dp", "fsdp"), None, None),
        P(("dp", "fsdp"), None),
        P(("dp", "fsdp"), None, None),
        P(("dp", "fsdp"), None),
        P(("dp", "fsdp"), None),
        P(("dp", "fsdp"), None),
        P(("dp", "fsdp"), None),
        P(("dp", "fsdp")),
        P(("dp", "fsdp")),
        P(("dp", "fsdp")),
        P(("dp", "fsdp")),
        P(("dp", "fsdp")),
        P(("dp", "fsdp")),
        P(("dp", "fsdp")),
        P(("dp", "fsdp")),
        P(("dp", "fsdp")),
        P(),
        P(),
        P(),
        P(),
    )
    out_specs = (P(("dp", "fsdp"), None, None), P(("dp", "fsdp"), None, None), P(), P(), P(), P())
    return jax.shard_map(local, mesh=mesh, in_specs=in_specs, out_specs=out_specs, check_vma=False)
```

profile of v0, /device:TPU:8, one launch (start us, length us, event | category | flops | bytes accessed | tf_op | source)
XLA Modules:
  0.0 645.6 jit_solution(10639014909072017310)
XLA Ops:
  11.6 57.1 %all-gather = bf16[32,24,8]{1,2,0:T(8,128)(2,1)S(1)} all-gather(bf16[1,24,8]{1,2,0:T(8,128)(2,1)S(1)} %bitcast.216), channel_id=1, replica_groups=mesh['dp'=8,'fsdp'=4] {'dp','fsdp'}, dimensions={0}, use_global_device_ids=true | all-gather | bytes 12672 | tf_op jit(solution)/shard_map/all_gather | solution.py:30
  73.8 50.2 %all-reduce = bf16[3072]{0:T(1024)(128)(2,1)S(1)} all-reduce(bf16[3072]{0:T(1024)(128)(2,1)S(1)} %dynamic-update-slice), channel_id=1, replica_groups=mesh['dp'=8,'fsdp'=4] {'dp','fsdp'}, use_global_device_ids=true, to_apply=%add | all-reduce | flops 3072 | bytes 12288
  124.7 51.4 %all-gather.1 = bf16[32,24,2]{1,2,0:T(2,128)(2,1)S(1)} all-gather(bf16[1,24,2]{1,2,0:T(2,128)(2,1)S(1)} %maximum_bitcast_fusion), channel_id=1, replica_groups=mesh['dp'=8,'fsdp'=4] {'dp','fsdp'}, dimensions={0}, use_global_device_ids=true | all-gather | bytes 3168 | tf_op jit(solution)/shard_map/all_gather | solution.py:41
  177.0 5.8 fusion.157
  183.0 3.4 copy-done.11
  186.5 2.7 fusion.122
  189.1 2.2 copy.92
  191.3 2.4 reshape.185
  193.7 2.9 copy.95
  196.6 4.6 fusion.120
  202.9 2.4 reshape.186
  208.6 3.8 reshape.187
  214.2 23.0 %while.26 = (s32[]{:T(128)}, bf16[2,512,12,64]{1,3,2,0:T(8,128)(2,1)}, f32[2,12,512]{2,1,0:T(8,128)}, bf16[2,512,12,64]{1,3,2,0:T(8,128)(2,1)}, s32[2,512]{1,0:T...) while((s32[]{:T(128)}, ...), condition=%wide.region_3.4_spmd, body=%wide.region_0.3_spmd.sunk | while | flops 849602560 | bytes 49250932 | solution.py:156
  217.2 3.1 fusion.217
  221.0 4.6 bitcast_dynamic-update-slice_fusion.4
  228.6 3.1 fusion.217
  232.4 4.6 bitcast_dynamic-update-slice_fusion.4
  237.2 3.0 copy.98
  241.8 3.9 fusion.155
  248.0 36.6 %fusion.103 = (f32[1024,3072]{1,0:T(8,128)}, f32[1024,3072]{1,0:T(8,128)}) fusion(f32[3072]{0:T(1024)S(1)} %copy-done.29, bf16[768,3072]{1,0:T(8,128)(2,1)} %all-gather.11.cloned.1.call-done, f32[1024,768]{1,0:T(8,128)} %copy-done.7, f32[768]{0:T(1024)S(1)} %copy-done.31, f32[768]{0:T(1024)S(1)} %copy-done.32, f32[1024]{0:T(1024)S(1)} %fusion.144, ...), kind=kOutput, calls=%fused_computation.80 | convolution fusion | flops 5033951232 | bytes 33056768 | tf_op jit(solution)/shard_map/dot_general | solution.py:166
  284.6 16.2 %fusion.156 = (f32[1024]{0:T(1024)S(1)}, f32[1024,768]{1,0:T(8,128)S(1)}) fusion(f32[768]{0:T(1024)S(1)} %copy-done.30, bf16[3072,768]{1,0:T(8,128)(2,1)} %all-gather.13.cloned.1.call-done, f32[1024,3072]{1,0:T(8,128)} %get-tuple-element.232, f32[1024,3072]{1,0:T(8,128)} %get-tuple-element.233, f32[3072]{0:T(1024)S(1)} %copy-done.29, ...), kind=kOutput, calls=%fused_computation.183 | convolution fusion | flops 4849925120 | bytes 36209664 | tf_op jit(solution)/shard_map/dot_general | solution.py:172
  301.9 3.2 fusion.154
  305.2 23.1 %multiply_reduce_fusion.1 = (f32[1024]{0:T(1024)S(1)}, f32[1024,768]{1,0:T(8,128)}) fusion(f32[1024,768]{1,0:T(8,128)} %copy-done.7, f32[1024]{0:T(1024)S(1)} %broadcast_multiply_fusion.1, f32[768]{0:T(1024)S(1)} %copy-done.34, bf16[768,3072]{1,0:T(8,128)(2,1)} %all-gather.11.cloned.1.call-done, f32[1024,3072]{1,0:T(8,128)} %get-tuple-element.232, ...), kind=kOutput, calls=%fused_computation.126 | convolution fusion | flops 9717152768 | bytes 44067840 | tf_op jit(solution)/shard_map/dot_general | solution.py:189
  328.3 3.6 fusion.153
  333.7 2.6 convolution_convert_fusion
  336.3 2.6 copy.101
  338.9 3.8 reshape.189
  342.7 2.9 copy.104
  345.6 126.3 %while.27 = (s32[]{:T(128)}, bf16[2,512,12,64]{1,3,2,0:T(8,128)(2,1)}, bf16[2,512,12,64]{1,3,2,0:T(8,128)(2,1)}, bf16[2,512,12,64]{1,3,2,0:T(8,128)(2,1)}, bf16[...) while((s32[]{:T(128)}, ...), condition=%wide.region_14.15_spmd, body=%wide.region_12.14_spmd.sunk | while | flops 2096509952 | bytes 160648368 | solution.py:197
  345.8 6.4 fusion.229
  352.2 6.3 fusion.228
  360.2 20.3 %fusion.231 = bf16[2,512,12,64]{1,3,2,0:T(8,128)(2,1)} fusion(bf16[2,512,12,64]{1,3,2,0:T(8,128)(2,1)} %get-tuple-element.383, s32[]{:T(128)} %get-tuple-element.381, f32[12,512,512]{1,2,0:T(8,128)} %fusion.228, f32[12,512,512]{1,2,0:T(8,128)} %fusion.229, f32[12,512]{1,0:T(8,128)S(1)} %dynamic-slice_bitcast_fusion.2, ...), kind=kOutput, calls=%fused_computation.44.clone.1 | convolution fusion | flops 437656064 | bytes 52495360 | tf_op jit(solution)/shard_map/while/body/eval_jaxpr/hqk,qhd->khd/dot_general | solution.py:84
  380.5 20.1 %fusion.230 = bf16[2,512,12,64]{1,3,2,0:T(8,128)(2,1)} fusion(bf16[2,512,12,64]{1,3,2,0:T(8,128)(2,1)} %get-tuple-element.382, s32[]{:T(128)} %get-tuple-element.381, f32[12,512,512]{1,2,0:T(8,128)} %fusion.228, f32[12,512,512]{1,2,0:T(8,128)} %fusion.229, f32[12,512]{1,0:T(8,128)S(1)} %dynamic-slice_bitcast_fusion.2, ...), kind=kOutput, calls=%fused_computation.46.clone.1 | convolution fusion | flops 437656064 | bytes 52495360 | tf_op jit(solution)/shard_map/while/body/eval_jaxpr/hqk,khd->qhd/dot_general | solution.py:81
  400.6 8.3 %fusion.232 = bf16[2,512,12,64]{1,3,2,0:T(8,128)(2,1)} fusion(bf16[2,512,12,64]{1,3,2,0:T(8,128)(2,1)} %get-tuple-element.384, s32[]{:T(128)} %get-tuple-element.381, f32[12,512,512]{1,2,0:T(8,128)} %fusion.229, f32[12,512]{1,0:T(8,128)S(1)} %dynamic-slice_bitcast_fusion.2, pred[512,512]{0,1:T(8,128)(4,1)S(1)} %broadcast_compare_fusion.5, ...), kind=kOutput, calls=%fused_computation.48.clone.1 | convolution fusion | flops 415629312 | bytes 14443520 | tf_op jit(solution)/shard_map/while/body/eval_jaxpr/hqk,qhd->khd/dot_general | solution.py:73
  408.9 6.4 fusion.229
  415.3 6.3 fusion.228
  423.3 20.3 %fusion.231 = bf16[2,512,12,64]{1,3,2,0:T(8,128)(2,1)} fusion(bf16[2,512,12,64]{1,3,2,0:T(8,128)(2,1)} %get-tuple-element.383, s32[]{:T(128)} %get-tuple-element.381, f32[12,512,512]{1,2,0:T(8,128)} %fusion.228, f32[12,512,512]{1,2,0:T(8,128)} %fusion.229, f32[12,512]{1,0:T(8,128)S(1)} %dynamic-slice_bitcast_fusion.2, ...), kind=kOutput, calls=%fused_computation.44.clone.1 | convolution fusion | flops 437656064 | bytes 52495360 | tf_op jit(solution)/shard_map/while/body/eval_jaxpr/hqk,qhd->khd/dot_general | solution.py:84
  443.6 20.1 %fusion.230 = bf16[2,512,12,64]{1,3,2,0:T(8,128)(2,1)} fusion(bf16[2,512,12,64]{1,3,2,0:T(8,128)(2,1)} %get-tuple-element.382, s32[]{:T(128)} %get-tuple-element.381, f32[12,512,512]{1,2,0:T(8,128)} %fusion.228, f32[12,512,512]{1,2,0:T(8,128)} %fusion.229, f32[12,512]{1,0:T(8,128)S(1)} %dynamic-slice_bitcast_fusion.2, ...), kind=kOutput, calls=%fused_computation.46.clone.1 | convolution fusion | flops 437656064 | bytes 52495360 | tf_op jit(solution)/shard_map/while/body/eval_jaxpr/hqk,khd->qhd/dot_general | solution.py:81
  463.7 8.3 %fusion.232 = bf16[2,512,12,64]{1,3,2,0:T(8,128)(2,1)} fusion(bf16[2,512,12,64]{1,3,2,0:T(8,128)(2,1)} %get-tuple-element.384, s32[]{:T(128)} %get-tuple-element.381, f32[12,512,512]{1,2,0:T(8,128)} %fusion.229, f32[12,512]{1,0:T(8,128)S(1)} %dynamic-slice_bitcast_fusion.2, pred[512,512]{0,1:T(8,128)(4,1)S(1)} %broadcast_compare_fusion.5, ...), kind=kOutput, calls=%fused_computation.48.clone.1 | convolution fusion | flops 415629312 | bytes 14443520 | tf_op jit(solution)/shard_map/while/body/eval_jaxpr/hqk,qhd->khd/dot_general | solution.py:73
  472.0 3.0 copy.108
  480.6 2.9 copy.109
  486.7 3.1 fusion.160
  489.8 2.4 fusion.126
  492.2 2.4 fusion.129
  495.9 3.1 copy.107
  500.7 6.6 %fusion.113 = f32[1024,768]{1,0:T(8,128)S(1)} fusion(bf16[768,2304]{1,0:T(8,128)(2,1)} %all-gather.7.cloned.1.call-done, bf16[1024,768]{0,1:T(8,128)(2,1)S(1)} %bitcast.200, bf16[1024,768]{0,1:T(8,128)(2,1)} %bitcast.210, bf16[1024,768]{0,1:T(8,128)(2,1)S(1)} %bitcast.203), kind=kOutput, calls=%fused_computation.102 | convolution fusion | flops 3638034432 | bytes 11403264 | tf_op jit(solution)/shard_map/dot_general | solution.py:219
  507.3 3.5 add_add_fusion.2
  510.8 122.5 %all-reduce.4.cloned.1.call-done = (f32[768,8]{0,1:T(8,128)}, f32[8,768]{1,0:T(8,128)}, f32[768,8]{0,1:T(8,128)}, f32[8,768]{1,0:T(8,128)}) async-done(((f32[768,8]{0,1:T(8,128)}, f32[8,768]{1,0:T(8,128)}, f32[768,8]{0,1:T(8,128)}, f32[8,768]{1,0:T(8,128)}), (f32[768,8]{0,1:T(8,128)}, f32[8,768]{1,0:T(8,128)}, f32[768,8]{0,1:T(8,128)}, f32[8,768]{1,0:T(8,128)})) %all-reduce.4.cloned.1.call-update) | async-done | bytes 98320 | tf_op jit(solution)/shard_map/psum | solution.py:238
  (155 shorter events, 52.1 us)
Async XLA Ops:
  7.2 179.3 %copy-start = (bf16[8,768]{1,0:T(8,128)(2,1)S(1)}, bf16[8,768]{1,0:T(8,128)(2,1)}, u32[]{:S(2)}) copy-start(bf16[8,768]{1,0:T(8,128)(2,1)} %param.43) | copy-start | bytes 36868
  7.2 169.8 %copy-start.1 = (bf16[2,512,768]{2,1,0:T(8,128)(2,1)S(1)}, bf16[2,512,768]{2,1,0:T(8,128)(2,1)}, u32[]{:S(2)}) copy-start(bf16[2,512,768]{2,1,0:T(8,128)(2,1)} %param.24) | copy-start | bytes 4718596
  7.2 66.4 %copy-start.36 = (bf16[96]{0:T(256)(128)(2,1)S(1)}, bf16[96]{0:T(256)(128)(2,1)}, u32[]{:S(2)}) copy-start(bf16[96]{0:T(256)(128)(2,1)} %param.36) | copy-start | bytes 580
  7.2 169.8 %all-gather.7.cloned.1.call-start = ((), (), s32[]{:S(2)}) async-start(), calls=%async_computation | async-start | bytes 3649536 | tf_op jit(solution)/shard_map/all_gather | solution.py:26
  7.9 233.8 %all-gather.9.cloned.1.call-start = ((), (), s32[]{:S(2)}) async-start(), calls=%async_computation.1 | async-start | bytes 1216512 | tf_op jit(solution)/shard_map/all_gather | solution.py:27
  8.7 239.2 %all-gather.11.cloned.1.call-start = ((), (), s32[]{:S(2)}) async-start(), calls=%async_computation.2 | async-start | bytes 4866048 | tf_op jit(solution)/shard_map/all_gather | solution.py:28
  9.4 275.1 %all-gather.13.cloned.1.call-start = ((), (), s32[]{:S(2)}) async-start(), calls=%async_computation.3 | async-start | bytes 4866048 | tf_op jit(solution)/shard_map/all_gather | solution.py:29
  10.0 623.3 %all-reduce.4.cloned.1.call-start = ((), (), s32[]{:S(2)}) async-start(), calls=%async_computation.4 | async-start | bytes 196608 | tf_op jit(solution)/shard_map/psum | solution.py:238
  71.6 111.4 %copy-start.18 = (f32[1024,8]{0,1:T(8,128)}, f32[1024,8]{0,1:T(8,128)S(1)}, u32[]{:S(2)}) copy-start(f32[1024,8]{0,1:T(8,128)S(1)} %fusion.158) | copy-start | bytes 98308
  73.5 123.0 %copy-start.16 = (f32[1024,8]{0,1:T(8,128)}, f32[1024,8]{0,1:T(8,128)S(1)}, u32[]{:S(2)}) copy-start(f32[1024,8]{0,1:T(8,128)S(1)} %fusion.159) | copy-start | bytes 98308
  182.8 3.6 copy-start.11
  191.3 5.3 copy-start.20
  217.2 3.8 copy-start.3
  228.6 3.8 copy-start.3
  237.1 4.6 copy-start.33
  245.7 1.7 copy-start.7
  245.7 2.2 copy-start.29
  245.7 2.2 copy-start.31
  245.7 2.2 copy-start.32
  247.9 36.6 %copy-start.30 = (f32[768]{0:T(1024)S(1)}, f32[768]{0:T(1024)}, u32[]{:S(2)}) copy-start(f32[768]{0:T(1024)} %get-tuple-element.175) | copy-start | bytes 9220
  284.6 16.3 %copy-start.12 = (bf16[2,512,768]{2,1,0:T(8,128)(2,1)S(1)}, bf16[2,512,768]{2,1,0:T(8,128)(2,1)}, u32[]{:S(2)}) copy-start(bf16[2,512,768]{2,1,0:T(8,128)(2,1)} %param.26) | copy-start | bytes 4718596
  284.6 16.3 %copy-start.24 = (f32[768]{0:T(1024)S(1)}, f32[768]{0:T(1024)}, u32[]{:S(2)}) copy-start(f32[768]{0:T(1024)} %get-tuple-element.182) | copy-start | bytes 9220
  300.8 1.1 copy-start.25
  300.8 1.1 copy-start.26
  301.9 3.3 copy-start.34
  328.3 5.3 copy-start.35
  331.9 1.8 copy-start.9
  331.9 1.7 copy-start.27
  345.8 6.4 copy-start.4
  345.8 6.4 copy-start.5
  408.9 6.4 copy-start.4
  408.9 6.4 copy-start.5
  475.4 1.9 copy-start.15
  478.9 4.5 copy-start.21
  480.6 4.8 copy-start.2
  480.6 6.1 copy-start.22
  483.5 6.3 copy-start.13
  483.5 6.3 copy-start.19
  485.4 6.8 %copy-start.14 = (bf16[1024,768]{1,0:T(8,128)(2,1)S(1)}, bf16[1024,768]{1,0:T(8,128)(2,1)}, u32[]{:S(2)}) copy-start(bf16[1024,768]{1,0:T(8,128)(2,1)} %copy.109) | copy-start | bytes 4718596
  485.4 6.8 %copy-start.17 = (f32[1024,8]{0,1:T(8,128)S(1)}, f32[1024,8]{0,1:T(8,128)}, u32[]{:S(2)}) copy-start(f32[1024,8]{0,1:T(8,128)} %copy-done.16) | copy-start | bytes 98308
  495.9 4.8 copy-start.6
  500.7 6.6 %copy-start.8 = (f32[1024,768]{1,0:T(8,128)S(1)}, f32[1024,768]{1,0:T(8,128)}, u32[]{:S(2)}) copy-start(f32[1024,768]{1,0:T(8,128)} %fusion.160) | copy-start | bytes 9437188
  500.7 6.6 %copy-start.10 = (f32[1024,768]{1,0:T(8,128)S(1)}, f32[1024,768]{1,0:T(8,128)}, u32[]{:S(2)}) copy-start(f32[1024,768]{1,0:T(8,128)} %copy-done.9) | copy-start | bytes 9437188
  500.7 6.6 %copy-start.23 = (bf16[768,8]{0,1:T(8,128)(2,1)S(1)}, bf16[768,8]{0,1:T(8,128)(2,1)}, u32[]{:S(2)}) copy-start(bf16[768,8]{0,1:T(8,128)(2,1)} %param.42) | copy-start | bytes 36868
  500.7 6.6 %copy-start.28 = (f32[1024]{0:T(1024)S(1)}, f32[1024]{0:T(1024)}, u32[]{:S(2)}) copy-start(f32[1024]{0:T(1024)} %copy-done.27) | copy-start | bytes 12292
Sparse Core Ops, SparseCore 0:
  10.9 61.1 all-gather.6
  75.0 52.4 all-gather.8
  130.4 64.2 all-gather.10
  197.4 62.3 all-gather.12
  500.8 132.4 all-reduce.3
where the time goes:
time: 652 us; the launch traced here: 646 us
  matrix products  258 us (40%)
  blocking collectives  159 us (24%)
  waiting for transfers between devices  125 us (19%)
  local copies, waits for them, and re-layouts  70 us (11%)
  other arithmetic  18.1 us (3%)
  between operations  14.7 us (2%)
    psum x1, waiting for transfers between devices, local(): lax.psum((term_query_down, term_query_up, term_value_down, term_value_up)...  123 us
    all_gather x1, blocking collectives, fetch_forward(): lax.all_gather(vectors, ('dp', 'fsdp'), axis=1, tiled=True)  57.1 us
    all_gather x1, blocking collectives, fetch_backward(): lax.all_gather(gains, ('dp', 'fsdp'), axis=1, tiled=True)  51.4 us
    unnamed x1, blocking collectives  50.2 us
    dot_general x2, matrix products, attend_back(): jnp.einsum('hqk,qhd->khd', grad_raw, query_rows, preferred_element_type=j...  40.7 us
    dot_general x2, matrix products, attend_back(): jnp.einsum('hqk,khd->qhd', grad_raw, key_rows, preferred_element_type=jnp...  40.1 us
    dot_general x1, matrix products, local(): jnp.dot(normed_one.astype(jnp.bfloat16), up_full, preferred_element_type=...  36.6 us
    dot_general x1, matrix products, local(): jnp.dot(grad_upper.astype(jnp.bfloat16), up_back.T, preferred_element_typ...  23.1 us
  transfers between devices with their start and end apart: 5, of which 1 were waited for; matrix products, arithmetic and copies ran while one was open for 19% of the time, Pallas kernels for 0%

commit v1 on v0

--- a/solution.py
+++ b/solution.py
@@ -9,6 +9,25 @@
 highest_precision_mode = lax.Precision.HIGHEST
 norm_epsilon = 1e-05
 adapter_scale = 2.0
+
+
+def _lay_cube(inp, link_axis):
+    r1, state_now, low = (lax.axis_size(link_axis), lax.axis_index(link_axis), inp.shape[1])
+    local_next, placed = (inp, 1)
+    while placed < r1:
+        local_next = jnp.concatenate(
+            [
+                local_next,
+                lax.ppermute(
+                    local_next,
+                    axis_name=link_axis,
+                    perm=[(idx, (idx - placed) % r1) for idx in range(r1)],
+                ),
+            ],
+            axis=1,
+        )
+        placed = 2 * placed
+    return jnp.roll(local_next, state_now * low, axis=1)
 
 
 def layer_norm(value_rows, gain, shift):
@@ -38,7 +57,7 @@
         lax.all_gather(out_weight, ("dp", "fsdp"), axis=0, tiled=True),
         lax.all_gather(up_weight, ("dp", "fsdp"), axis=0, tiled=True),
         lax.all_gather(down_weight, ("dp", "fsdp"), axis=0, tiled=True),
-        lax.all_gather(gains, ("dp", "fsdp"), axis=1, tiled=True),
+        _lay_cube(gains, ("dp", "fsdp")),
     )
 
 

time: 652 us -> 620 us (0.951)
  blocking collectives: 159 us -> 96.9 us
  starting transfers between devices: 0.19 us -> 19 us
  waiting for transfers between devices: 125 us -> 133 us
    all_gather x1 -> x0, blocking collectives: 51.4 us -> none  [fetch_backward(): lax.all_gather(gains, ('dp', 'fsdp'), axis=1, tiled=True)]
    ppermute x0 -> x5, starting transfers between devices: none -> 18.8 us  [_lay_cube(): lax.ppermute(local_next, axis_name=link_axis, perm=[(idx, (idx - placed)...]
    all_gather x1, waiting for transfers between devices: 0.01 us -> 14.5 us  [fetch_forward(): lax.all_gather(down_weight, ('dp', 'fsdp'), axis=0, tiled=True)]
    psum x1, waiting for transfers between devices: 123 us -> 112 us  [local(): lax.psum((term_query_down, term_query_up, term_value_down, term_value_up)...]
    unnamed x1, blocking collectives: 50.2 us -> 41.1 us
    unnamed x78 -> x82, local copies, waits for them, and re-layouts: 17.8 us -> 17.8 us
  transfers between devices with their start and end apart: 5 -> 10, of which waited for: 1 -> 5; matrix products, arithmetic and copies ran while one was open for 19% -> 20% of each run, Pallas kernels for 0% -> 0%
where the time goes in v1:
time: 620 us; the launch traced here: 610 us
  matrix products  258 us (42%)
  waiting for transfers between devices  133 us (21%)
  blocking collectives  96.9 us (16%)
  local copies, waits for them, and re-layouts  69.2 us (11%)
  starting transfers between devices  19 us (3%)
  other arithmetic  18.8 us (3%)
  between operations  14.7 us (2%)
    psum x1, waiting for transfers between devices, local(): lax.psum((term_query_down, term_query_up, term_value_down, term_value_up)...  112 us
    all_gather x1, blocking collectives, fetch_forward(): lax.all_gather(vectors, ('dp', 'fsdp'), axis=1, tiled=True)  55.8 us
    unnamed x1, blocking collectives  41.1 us
    dot_general x2, matrix products, attend_back(): jnp.einsum('hqk,qhd->khd', grad_raw, query_rows, preferred_element_type=j...  40.5 us
    dot_general x2, matrix products, attend_back(): jnp.einsum('hqk,khd->qhd', grad_raw, key_rows, preferred_element_type=jnp...  40.1 us
    dot_general x1, matrix products, local(): jnp.dot(normed_one.astype(jnp.bfloat16), up_full, preferred_element_type=...  36.8 us
    dot_general x1, matrix products, local(): jnp.dot(grad_upper.astype(jnp.bfloat16), up_back.T, preferred_element_typ...  23.1 us
    ppermute x5, starting transfers between devices, _lay_cube(): lax.ppermute(local_next, axis_name=link_axis, perm=[(idx, (idx - placed)...  18.8 us
  transfers between devices with their start and end apart: 10, of which 5 were waited for; matrix products, arithmetic and copies ran while one was open for 20% of the time, Pallas kernels for 0%

profile of v1, /device:TPU:8, one launch (start us, length us, event | category | flops | bytes accessed | tf_op | source)
XLA Modules:
  0.0 610.1 jit_solution(5498351245723242659)
XLA Ops:
  12.9 55.8 %all-gather = bf16[32,24,8]{1,2,0:T(8,128)(2,1)S(1)} all-gather(bf16[1,24,8]{1,2,0:T(8,128)(2,1)S(1)} %bitcast.208), channel_id=1, replica_groups=mesh['dp'=8,'fsdp'=4] {'dp','fsdp'}, dimensions={0}, use_global_device_ids=true | all-gather | bytes 12672 | tf_op jit(solution)/shard_map/all_gather | solution.py:49
  73.7 3.8 collective-permute-start.1
  78.8 6.2 %collective-permute-start.2 = (bf16[2,96]{1,0:T(2,128)(2,1)S(1)}, bf16[2,96]{1,0:T(2,128)(2,1)S(1)}, u32[]{:S(2)}, u32[]{:S(2)}) collective-permute-start(bf16[2,96]{1,0:T(2,128)(2,1)S(1)} %pad_maximum_fusion.3), channel_id=1, source_target_pairs={{0,28},{1,29},{2,30},{3,31},{4,0},{5,1},{6,2},{7,3},{8,4},{9,5},{1... | collective-permute-start | bytes 1160 | tf_op jit(solution)/shard_map/ppermute | solution.py:21
  86.4 4.4 collective-permute-start.3
  92.2 2.7 collective-permute-start.4
  94.8 41.1 %all-reduce = bf16[3072]{0:T(1024)(128)(2,1)S(1)} all-reduce(bf16[3072]{0:T(1024)(128)(2,1)S(1)} %dynamic-update-slice), channel_id=1, replica_groups=mesh['dp'=8,'fsdp'=4] {'dp','fsdp'}, use_global_device_ids=true, to_apply=%add | all-reduce | flops 3072 | bytes 12288
  137.4 5.9 fusion.157
  143.5 3.4 copy-done.11
  146.9 2.7 fusion.122
  151.3 2.4 reshape.185
  153.7 2.9 copy.93
  156.6 4.6 fusion.120
  168.6 3.8 reshape.187
  174.2 23.0 %while.26 = (s32[]{:T(128)}, bf16[2,512,12,64]{1,3,2,0:T(8,128)(2,1)}, f32[2,12,512]{2,1,0:T(8,128)}, bf16[2,512,12,64]{1,3,2,0:T(8,128)(2,1)}, s32[2,512]{1,0:T...) while((s32[]{:T(128)}, ...), condition=%wide.region_3.4_spmd, body=%wide.region_0.3_spmd.sunk | while | flops 849602560 | bytes 49250932 | solution.py:175
  177.4 3.1 fusion.217
  181.2 4.6 bitcast_dynamic-update-slice_fusion.4
  188.8 3.1 fusion.217
  192.6 4.6 bitcast_dynamic-update-slice_fusion.4
  197.2 3.0 copy.96
  201.8 4.0 fusion.155
  208.1 36.8 %fusion.103 = (f32[1024,3072]{1,0:T(8,128)}, f32[1024,3072]{1,0:T(8,128)}) fusion(f32[3072]{0:T(1024)S(1)} %copy-done.29, bf16[768,3072]{1,0:T(8,128)(2,1)} %all-gather.10.cloned.1.call-done, f32[1024,768]{1,0:T(8,128)} %copy-done.7, f32[768]{0:T(1024)S(1)} %copy-done.33, f32[768]{0:T(1024)S(1)} %copy-done.34, f32[1024]{0:T(1024)S(1)} %fusion.144, ...), kind=kOutput, calls=%fused_computation.80 | convolution fusion | flops 5033951232 | bytes 33056768 | tf_op jit(solution)/shard_map/dot_general | solution.py:185
  244.9 14.5 %all-gather.12.cloned.1.call-done = bf16[3072,768]{1,0:T(8,128)(2,1)} async-done(((bf16[96,768]{1,0:T(8,128)(2,1)}), bf16[3072,768]{1,0:T(8,128)(2,1)}) %all-gather.12.cloned.1.call-update) | async-done | bytes 4718608 | tf_op jit(solution)/shard_map/all_gather | solution.py:48
  259.4 15.9 %fusion.156 = (f32[1024]{0:T(1024)S(1)}, f32[1024,768]{1,0:T(8,128)S(1)}) fusion(f32[768]{0:T(1024)S(1)} %copy-done.32, bf16[3072,768]{1,0:T(8,128)(2,1)} %all-gather.12.cloned.1.call-done, f32[1024,3072]{1,0:T(8,128)} %get-tuple-element.232, f32[1024,3072]{1,0:T(8,128)} %get-tuple-element.233, f32[3072]{0:T(1024)S(1)} %copy-done.29, ...), kind=kOutput, calls=%fused_computation.187 | convolution fusion | flops 4849925120 | bytes 36209664 | tf_op jit(solution)/shard_map/dot_general | solution.py:191
  276.4 3.6 fusion.154
  280.0 23.1 %multiply_reduce_fusion.1 = (f32[1024]{0:T(1024)S(1)}, f32[1024,768]{1,0:T(8,128)}) fusion(f32[1024,768]{1,0:T(8,128)} %copy-done.7, f32[1024]{0:T(1024)S(1)} %broadcast_multiply_fusion.1, f32[768]{0:T(1024)S(1)} %copy-done.36, bf16[768,3072]{1,0:T(8,128)(2,1)} %all-gather.10.cloned.1.call-done, f32[1024,3072]{1,0:T(8,128)} %get-tuple-element.232, ...), kind=kOutput, calls=%fused_computation.126 | convolution fusion | flops 9717152768 | bytes 44067840 | tf_op jit(solution)/shard_map/dot_general | solution.py:208
  303.1 3.6 fusion.153
  308.5 2.6 convolution_convert_fusion
  311.1 2.6 copy.97
  313.7 3.8 reshape.189
  317.5 2.9 copy.100
  320.4 126.4 %while.27 = (s32[]{:T(128)}, bf16[2,512,12,64]{1,3,2,0:T(8,128)(2,1)}, bf16[2,512,12,64]{1,3,2,0:T(8,128)(2,1)}, bf16[2,512,12,64]{1,3,2,0:T(8,128)(2,1)}, bf16[...) while((s32[]{:T(128)}, ...), condition=%wide.region_14.15_spmd, body=%wide.region_12.14_spmd.sunk | while | flops 2096509952 | bytes 160648368 | solution.py:216
  320.6 6.4 %fusion.229 = f32[12,512,512]{1,2,0:T(8,128)} fusion(bf16[2,512,12,64]{1,3,2,0:T(8,128)(2,1)S(1)} %get-tuple-element.398, s32[]{:T(128)} %get-tuple-element.381, bf16[2,512,12,64]{1,3,2,0:T(8,128)(2,1)S(1)} %get-tuple-element.396), kind=kOutput, calls=%fused_computation.54.clone.1 | convolution fusion | flops 402653184 | bytes 14156800 | tf_op jit(solution)/shard_map/while/body/eval_jaxpr/qhd,khd->hqk/dot_general | solution.py:87
  327.0 6.3 %fusion.228 = f32[12,512,512]{1,2,0:T(8,128)} fusion(bf16[2,512,12,64]{1,3,2,0:T(8,128)(2,1)S(1)} %copy-done.4, s32[]{:T(128)} %get-tuple-element.381, bf16[2,512,12,64]{1,3,2,0:T(8,128)(2,1)S(1)} %copy-done.5), kind=kOutput, calls=%fused_computation.49.clone.1 | convolution fusion | flops 402653184 | bytes 14156800 | tf_op jit(solution)/shard_map/while/body/eval_jaxpr/qhd,khd->hqk/dot_general | solution.py:95
  335.0 20.3 %fusion.231 = bf16[2,512,12,64]{1,3,2,0:T(8,128)(2,1)} fusion(bf16[2,512,12,64]{1,3,2,0:T(8,128)(2,1)} %get-tuple-element.383, s32[]{:T(128)} %get-tuple-element.381, f32[12,512,512]{1,2,0:T(8,128)} %fusion.228, f32[12,512,512]{1,2,0:T(8,128)} %fusion.229, f32[12,512]{1,0:T(8,128)S(1)} %dynamic-slice_bitcast_fusion.2, ...), kind=kOutput, calls=%fused_computation.44.clone.1 | convolution fusion | flops 437656064 | bytes 52495360 | tf_op jit(solution)/shard_map/while/body/eval_jaxpr/hqk,qhd->khd/dot_general | solution.py:103
  355.3 20.1 %fusion.230 = bf16[2,512,12,64]{1,3,2,0:T(8,128)(2,1)} fusion(bf16[2,512,12,64]{1,3,2,0:T(8,128)(2,1)} %get-tuple-element.382, s32[]{:T(128)} %get-tuple-element.381, f32[12,512,512]{1,2,0:T(8,128)} %fusion.228, f32[12,512,512]{1,2,0:T(8,128)} %fusion.229, f32[12,512]{1,0:T(8,128)S(1)} %dynamic-slice_bitcast_fusion.2, ...), kind=kOutput, calls=%fused_computation.46.clone.1 | convolution fusion | flops 437656064 | bytes 52495360 | tf_op jit(solution)/shard_map/while/body/eval_jaxpr/hqk,khd->qhd/dot_general | solution.py:100
  375.3 8.3 %fusion.232 = bf16[2,512,12,64]{1,3,2,0:T(8,128)(2,1)} fusion(bf16[2,512,12,64]{1,3,2,0:T(8,128)(2,1)} %get-tuple-element.384, s32[]{:T(128)} %get-tuple-element.381, f32[12,512,512]{1,2,0:T(8,128)} %fusion.229, f32[12,512]{1,0:T(8,128)S(1)} %dynamic-slice_bitcast_fusion.2, pred[512,512]{0,1:T(8,128)(4,1)S(1)} %broadcast_compare_fusion.5, ...), kind=kOutput, calls=%fused_computation.48.clone.1 | convolution fusion | flops 415629312 | bytes 14443520 | tf_op jit(solution)/shard_map/while/body/eval_jaxpr/hqk,qhd->khd/dot_general | solution.py:92
  383.6 6.4 %fusion.229 = f32[12,512,512]{1,2,0:T(8,128)} fusion(bf16[2,512,12,64]{1,3,2,0:T(8,128)(2,1)S(1)} %get-tuple-element.398, s32[]{:T(128)} %get-tuple-element.381, bf16[2,512,12,64]{1,3,2,0:T(8,128)(2,1)S(1)} %get-tuple-element.396), kind=kOutput, calls=%fused_computation.54.clone.1 | convolution fusion | flops 402653184 | bytes 14156800 | tf_op jit(solution)/shard_map/while/body/eval_jaxpr/qhd,khd->hqk/dot_general | solution.py:87
  390.0 6.3 %fusion.228 = f32[12,512,512]{1,2,0:T(8,128)} fusion(bf16[2,512,12,64]{1,3,2,0:T(8,128)(2,1)S(1)} %copy-done.4, s32[]{:T(128)} %get-tuple-element.381, bf16[2,512,12,64]{1,3,2,0:T(8,128)(2,1)S(1)} %copy-done.5), kind=kOutput, calls=%fused_computation.49.clone.1 | convolution fusion | flops 402653184 | bytes 14156800 | tf_op jit(solution)/shard_map/while/body/eval_jaxpr/qhd,khd->hqk/dot_general | solution.py:95
  398.0 20.3 %fusion.231 = bf16[2,512,12,64]{1,3,2,0:T(8,128)(2,1)} fusion(bf16[2,512,12,64]{1,3,2,0:T(8,128)(2,1)} %get-tuple-element.383, s32[]{:T(128)} %get-tuple-element.381, f32[12,512,512]{1,2,0:T(8,128)} %fusion.228, f32[12,512,512]{1,2,0:T(8,128)} %fusion.229, f32[12,512]{1,0:T(8,128)S(1)} %dynamic-slice_bitcast_fusion.2, ...), kind=kOutput, calls=%fused_computation.44.clone.1 | convolution fusion | flops 437656064 | bytes 52495360 | tf_op jit(solution)/shard_map/while/body/eval_jaxpr/hqk,qhd->khd/dot_general | solution.py:103
  418.3 20.0 %fusion.230 = bf16[2,512,12,64]{1,3,2,0:T(8,128)(2,1)} fusion(bf16[2,512,12,64]{1,3,2,0:T(8,128)(2,1)} %get-tuple-element.382, s32[]{:T(128)} %get-tuple-element.381, f32[12,512,512]{1,2,0:T(8,128)} %fusion.228, f32[12,512,512]{1,2,0:T(8,128)} %fusion.229, f32[12,512]{1,0:T(8,128)S(1)} %dynamic-slice_bitcast_fusion.2, ...), kind=kOutput, calls=%fused_computation.46.clone.1 | convolution fusion | flops 437656064 | bytes 52495360 | tf_op jit(solution)/shard_map/while/body/eval_jaxpr/hqk,khd->qhd/dot_general | solution.py:100
  438.3 8.3 %fusion.232 = bf16[2,512,12,64]{1,3,2,0:T(8,128)(2,1)} fusion(bf16[2,512,12,64]{1,3,2,0:T(8,128)(2,1)} %get-tuple-element.384, s32[]{:T(128)} %get-tuple-element.381, f32[12,512,512]{1,2,0:T(8,128)} %fusion.229, f32[12,512]{1,0:T(8,128)S(1)} %dynamic-slice_bitcast_fusion.2, pred[512,512]{0,1:T(8,128)(4,1)S(1)} %broadcast_compare_fusion.5, ...), kind=kOutput, calls=%fused_computation.48.clone.1 | convolution fusion | flops 415629312 | bytes 14443520 | tf_op jit(solution)/shard_map/while/body/eval_jaxpr/hqk,qhd->khd/dot_general | solution.py:92
  446.8 3.0 copy.104
  455.4 2.7 copy.105
  461.3 3.1 fusion.160
  470.5 3.1 copy.103
  475.3 6.6 %fusion.113 = f32[1024,768]{1,0:T(8,128)S(1)} fusion(bf16[768,2304]{1,0:T(8,128)(2,1)} %all-gather.6.cloned.1.call-done, bf16[1024,768]{0,1:T(8,128)(2,1)S(1)} %bitcast.193, bf16[1024,768]{0,1:T(8,128)(2,1)} %bitcast.203, bf16[1024,768]{0,1:T(8,128)(2,1)S(1)} %bitcast.196), kind=kOutput, calls=%fused_computation.102 | convolution fusion | flops 3638034432 | bytes 11403264 | tf_op jit(solution)/shard_map/dot_general | solution.py:238
  481.9 3.5 add_add_fusion.2
  485.4 112.4 %all-reduce.4.cloned.1.call-done = (f32[768,8]{0,1:T(8,128)}, f32[8,768]{1,0:T(8,128)}, f32[768,8]{0,1:T(8,128)}, f32[8,768]{1,0:T(8,128)}) async-done(((f32[768,8]{0,1:T(8,128)}, f32[8,768]{1,0:T(8,128)}, f32[768,8]{0,1:T(8,128)}, f32[8,768]{1,0:T(8,128)}), (f32[768,8]{0,1:T(8,128)}, f32[8,768]{1,0:T(8,128)}, f32[768,8]{0,1:T(8,128)}, f32[8,768]{1,0:T(8,128)})) %all-reduce.4.cloned.1.call-update) | async-done | bytes 98320 | tf_op jit(solution)/shard_map/psum | solution.py:257
  (171 shorter events, 66.1 us)
Async XLA Ops:
  7.2 139.8 %copy-start = (bf16[8,768]{1,0:T(8,128)(2,1)S(1)}, bf16[8,768]{1,0:T(8,128)(2,1)}, u32[]{:S(2)}) copy-start(bf16[8,768]{1,0:T(8,128)(2,1)} %param.43) | copy-start | bytes 36868
  7.2 66.4 %copy-start.30 = (bf16[24]{0:T(256)(128)(2,1)S(1)}, bf16[24]{0:T(256)(128)(2,1)}, u32[]{:S(2)}) copy-start(bf16[24]{0:T(256)(128)(2,1)} %param.34) | copy-start | bytes 148
  7.2 66.4 %copy-start.31 = (bf16[24]{0:T(256)(128)(2,1)S(1)}, bf16[24]{0:T(256)(128)(2,1)}, u32[]{:S(2)}) copy-start(bf16[24]{0:T(256)(128)(2,1)} %param.38) | copy-start | bytes 148
  7.2 130.2 %copy-start.1 = (bf16[2,512,768]{2,1,0:T(8,128)(2,1)S(1)}, bf16[2,512,768]{2,1,0:T(8,128)(2,1)}, u32[]{:S(2)}) copy-start(bf16[2,512,768]{2,1,0:T(8,128)(2,1)} %param.24) | copy-start | bytes 4718596
  7.2 83.6 %copy-start.38 = (bf16[96]{0:T(256)(128)(2,1)S(1)}, bf16[96]{0:T(256)(128)(2,1)}, u32[]{:S(2)}) copy-start(bf16[96]{0:T(256)(128)(2,1)} %param.36) | copy-start | bytes 580
  7.2 130.1 %all-gather.6.cloned.1.call-start = ((), (), s32[]{:S(2)}) async-start(), calls=%async_computation | async-start | bytes 3649536 | tf_op jit(solution)/shard_map/all_gather | solution.py:45
  8.0 193.8 %all-gather.8.cloned.1.call-start = ((), (), s32[]{:S(2)}) async-start(), calls=%async_computation.1 | async-start | bytes 1216512 | tf_op jit(solution)/shard_map/all_gather | solution.py:46
  8.7 199.3 %all-gather.10.cloned.1.call-start = ((), (), s32[]{:S(2)}) async-start(), calls=%async_computation.2 | async-start | bytes 4866048 | tf_op jit(solution)/shard_map/all_gather | solution.py:47
  9.4 249.9 %all-gather.12.cloned.1.call-start = ((), (), s32[]{:S(2)}) async-start(), calls=%async_computation.3 | async-start | bytes 4866048 | tf_op jit(solution)/shard_map/all_gather | solution.py:48
  10.2 63.4 %collective-permute-start = (bf16[2,24]{1,0:T(2,128)(2,1)S(1)}, bf16[2,24]{1,0:T(2,128)(2,1)S(1)}, u32[]{:S(2)}, u32[]{:S(2)}) collective-permute-start(bf16[2,24]{1,0:T(2,128)(2,1)S(1)} %pad_maximum_fusion.1), channel_id=1, source_target_pairs={{0,31},{1,0},{2,1},{3,2},{4,3},{5,4},{6,5},{7,6},{8,7},{9,8},{10,9... | collective-permute-start | bytes 296 | tf_op jit(solution)/shard_map/ppermute | solution.py:21
  12.0 585.8 %all-reduce.4.cloned.1.call-start = ((), (), s32[]{:S(2)}) async-start(), calls=%async_computation.4 | async-start | bytes 196608 | tf_op jit(solution)/shard_map/psum | solution.py:257
  71.6 71.9 %copy-start.18 = (f32[1024,8]{0,1:T(8,128)}, f32[1024,8]{0,1:T(8,128)S(1)}, u32[]{:S(2)}) copy-start(f32[1024,8]{0,1:T(8,128)S(1)} %fusion.158) | copy-start | bytes 98308
  73.5 83.0 %copy-start.16 = (f32[1024,8]{0,1:T(8,128)}, f32[1024,8]{0,1:T(8,128)S(1)}, u32[]{:S(2)}) copy-start(f32[1024,8]{0,1:T(8,128)S(1)} %fusion.159) | copy-start | bytes 98308
  73.7 5.1 collective-permute-start.1
  78.8 7.5 %collective-permute-start.2 = (bf16[2,96]{1,0:T(2,128)(2,1)S(1)}, bf16[2,96]{1,0:T(2,128)(2,1)S(1)}, u32[]{:S(2)}, u32[]{:S(2)}) collective-permute-start(bf16[2,96]{1,0:T(2,128)(2,1)S(1)} %pad_maximum_fusion.3), channel_id=1, source_target_pairs={{0,28},{1,29},{2,30},{3,31},{4,0},{5,1},{6,2},{7,3},{8,4},{9,5},{1... | collective-permute-start | bytes 1160 | tf_op jit(solution)/shard_map/ppermute | solution.py:21
  86.4 5.7 collective-permute-start.3
  92.2 44.4 %collective-permute-start.4 = (bf16[2,384]{1,0:T(2,128)(2,1)S(1)}, bf16[2,384]{1,0:T(2,128)(2,1)S(1)}, u32[]{:S(2)}, u32[]{:S(2)}) collective-permute-start(bf16[2,384]{1,0:T(2,128)(2,1)S(1)} %concatenate.28), channel_id=1, source_target_pairs={{0,16},{1,17},{2,18},{3,19},{4,20},{5,21},{6,22},{7,23},{8,24},{9,... | collective-permute-start | bytes 4616 | tf_op jit(solution)/shard_map/ppermute | solution.py:21
  143.3 3.6 copy-start.11
  151.3 5.3 copy-start.20
  177.4 3.8 copy-start.3
  188.8 3.8 copy-start.3
  197.2 4.6 copy-start.35
  205.8 2.2 copy-start.29
  205.8 2.2 copy-start.33
  205.8 2.2 copy-start.34
  208.0 51.3 %copy-start.32 = (f32[768]{0:T(1024)S(1)}, f32[768]{0:T(1024)}, u32[]{:S(2)}) copy-start(f32[768]{0:T(1024)} %get-tuple-element.175) | copy-start | bytes 9220
  259.4 15.9 %copy-start.12 = (bf16[2,512,768]{2,1,0:T(8,128)(2,1)S(1)}, bf16[2,512,768]{2,1,0:T(8,128)(2,1)}, u32[]{:S(2)}) copy-start(bf16[2,512,768]{2,1,0:T(8,128)(2,1)} %param.26) | copy-start | bytes 4718596
  259.4 15.9 %copy-start.24 = (f32[768]{0:T(1024)S(1)}, f32[768]{0:T(1024)}, u32[]{:S(2)}) copy-start(f32[768]{0:T(1024)} %get-tuple-element.182) | copy-start | bytes 9220
  276.4 3.7 copy-start.36
  303.1 5.3 copy-start.37
  306.7 1.8 copy-start.9
  320.6 6.4 %copy-start.4 = (bf16[2,512,12,64]{1,3,2,0:T(8,128)(2,1)S(1)}, bf16[2,512,12,64]{1,3,2,0:T(8,128)(2,1)}, u32[]{:S(2)}) copy-start(bf16[2,512,12,64]{1,3,2,0:T(8,128)(2,1)} %get-tuple-element.401) | copy-start | bytes 4718596 | tf_op jit(solution)/shard_map/while
  320.6 6.4 %copy-start.5 = (bf16[2,512,12,64]{1,3,2,0:T(8,128)(2,1)S(1)}, bf16[2,512,12,64]{1,3,2,0:T(8,128)(2,1)}, u32[]{:S(2)}) copy-start(bf16[2,512,12,64]{1,3,2,0:T(8,128)(2,1)} %get-tuple-element.400) | copy-start | bytes 4718596 | tf_op jit(solution)/shard_map/while
  383.6 6.4 %copy-start.4 = (bf16[2,512,12,64]{1,3,2,0:T(8,128)(2,1)S(1)}, bf16[2,512,12,64]{1,3,2,0:T(8,128)(2,1)}, u32[]{:S(2)}) copy-start(bf16[2,512,12,64]{1,3,2,0:T(8,128)(2,1)} %get-tuple-element.401) | copy-start | bytes 4718596 | tf_op jit(solution)/shard_map/while
  383.6 6.4 %copy-start.5 = (bf16[2,512,12,64]{1,3,2,0:T(8,128)(2,1)S(1)}, bf16[2,512,12,64]{1,3,2,0:T(8,128)(2,1)}, u32[]{:S(2)}) copy-start(bf16[2,512,12,64]{1,3,2,0:T(8,128)(2,1)} %get-tuple-element.400) | copy-start | bytes 4718596 | tf_op jit(solution)/shard_map/while
  450.3 1.9 copy-start.15
  453.8 4.3 copy-start.21
  455.4 4.6 copy-start.2
  455.4 5.9 copy-start.22
  458.1 6.3 %copy-start.13 = (bf16[1024,768]{1,0:T(8,128)(2,1)S(1)}, bf16[1024,768]{1,0:T(8,128)(2,1)}, u32[]{:S(2)}) copy-start(bf16[1024,768]{1,0:T(8,128)(2,1)} %copy.106) | copy-start | bytes 4718596
  458.1 6.3 %copy-start.19 = (f32[1024,8]{0,1:T(8,128)S(1)}, f32[1024,8]{0,1:T(8,128)}, u32[]{:S(2)}) copy-start(f32[1024,8]{0,1:T(8,128)} %copy-done.18) | copy-start | bytes 98308
  460.0 6.8 %copy-start.14 = (bf16[1024,768]{1,0:T(8,128)(2,1)S(1)}, bf16[1024,768]{1,0:T(8,128)(2,1)}, u32[]{:S(2)}) copy-start(bf16[1024,768]{1,0:T(8,128)(2,1)} %copy.105) | copy-start | bytes 4718596
  460.0 6.8 %copy-start.17 = (f32[1024,8]{0,1:T(8,128)S(1)}, f32[1024,8]{0,1:T(8,128)}, u32[]{:S(2)}) copy-start(f32[1024,8]{0,1:T(8,128)} %copy-done.16) | copy-start | bytes 98308
  470.5 4.8 copy-start.6
  475.3 6.6 %copy-start.8 = (f32[1024,768]{1,0:T(8,128)S(1)}, f32[1024,768]{1,0:T(8,128)}, u32[]{:S(2)}) copy-start(f32[1024,768]{1,0:T(8,128)} %fusion.160) | copy-start | bytes 9437188
  475.3 6.6 %copy-start.10 = (f32[1024,768]{1,0:T(8,128)S(1)}, f32[1024,768]{1,0:T(8,128)}, u32[]{:S(2)}) copy-start(f32[1024,768]{1,0:T(8,128)} %copy-done.9) | copy-start | bytes 9437188
  475.3 6.6 %copy-start.23 = (bf16[768,8]{0,1:T(8,128)(2,1)S(1)}, bf16[768,8]{0,1:T(8,128)(2,1)}, u32[]{:S(2)}) copy-start(bf16[768,8]{0,1:T(8,128)(2,1)} %param.42) | copy-start | bytes 36868
  475.3 6.6 %copy-start.28 = (f32[1024]{0:T(1024)S(1)}, f32[1024]{0:T(1024)}, u32[]{:S(2)}) copy-start(f32[1024]{0:T(1024)} %copy-done.27) | copy-start | bytes 12292
  (4 other events, 5.7 us)
Sparse Core Ops, SparseCore 0:
  11.0 61.0 all-gather.5
  74.9 52.4 all-gather.7
  130.3 63.7 all-gather.9
  196.9 62.4 all-gather.11
  475.4 122.3 all-reduce.3
